TPU v7x, 256 devices: a whole 4x4x8 slice. The times are simulated.
256 devices in a mesh: blk: 64 (over y_lo, z, x), rep: 4 (over y_hi, core).
Axes of the slice: x: 4, y: 4 (y_hi: 2, y_lo: 2; y = y_hi * 2 + y_lo), z: 8, core: 2. Of those that a mesh axis runs over, the one named last changes fastest.
Arguments:
- points: bfloat16 [49152, 1024], P('blk'), may hold values from -6 to 6
- w_in: bfloat16 [1024, 512], replicated, may hold values from -0.1875 to 0.1875
- b_in: float32 [512], replicated, may hold values from -3 to 3
- w_out: bfloat16 [512, 64], replicated, may hold values from -0.25 to 0.25
- inv_scale: float32 [64], replicated, may hold values from 0.05 to 0.5
- solves: bfloat16 [64, 49152], P(None, 'blk'), may hold values from -1 to 1
- probes: bfloat16 [64, 49152], P(None, 'blk'), may hold values from -1 to 1
Outputs:
- feat_grad: float32 [64, 49152], P(None, ('blk', 'rep'))
- grad_w_in: float32 [1024, 512], replicated
- grad_b_in: float32 [512], replicated
- grad_w_out: float32 [512, 64], replicated
All inputs are finite; a program needn't handle non-finite values.
Results may differ from a plain program's by a relative error of at most 0.034.
Values may be sent and summed in bfloat16 or wider, within the bound.
A program may use at most 64 MiB of HBM per device.

v0:
```python
import math
import jax
import jax.numpy as jnp
from jax import lax
from jax.sharding import PartitionSpec as P


def shifted(block, axis, distance):
    devices = range(lax.axis_size(axis))
    route = [((i - distance) % len(devices), i) for i in devices]
    return lax.ppermute(block, axis, route)


def cut_along(value, dim, count):
    lengths = value.shape
    blocks = value.reshape(*lengths[:dim], count, lengths[dim] // count, *lengths[dim + 1 :])
    return jnp.moveaxis(blocks, dim, 0)


def sum_at_owner(value, axis, dim):
    count = lax.axis_size(axis)
    blocks = lax.all_to_all(cut_along(value, dim, count), axis, 0, 0, tiled=True)
    return jnp.sum(blocks, axis=0)


def couple(own_y, own_pair, own_sq, visitor, feat):
    vis_y = visitor[:feat]
    vis_pair = visitor[feat:]
    vis_sq = jnp.sum(jnp.square(vis_y.astype(jnp.float32)), axis=0)
    cross = lax.dot_general(
        own_y, vis_y, (((0,), (0,)), ((), ())), preferred_element_type=jnp.float32
    )
    kernel = jnp.exp(-0.5 * (own_sq[:, None] + vis_sq[None, :] - 2.0 * cross))
    coupling = lax.dot_general(
        own_pair, vis_pair, (((0,), (0,)), ((), ())), preferred_element_type=jnp.float32
    )
    weight_b = (coupling * kernel).astype(jnp.bfloat16)
    totals = jnp.sum(weight_b.astype(jnp.float32), axis=1)
    pull = lax.dot_general(
        vis_y, weight_b, (((1,), (1,)), ((), ())), preferred_element_type=jnp.float32
    )
    return (totals, pull)


def on_device(points, w_in, b_in, w_out, inv_scale, solves, probes):
    feat = w_out.shape[1]
    reps = lax.axis_size("rep")
    blocks = lax.axis_size("blk")
    rep_index = lax.axis_index("rep")
    rows = points.shape[0]
    quarter = rows // reps
    first = rep_index * quarter
    npts = rows * blocks
    levels = reps.bit_length() - 1
    own_points = lax.dynamic_slice_in_dim(points, first, quarter, 0)
    hidden = jnp.tanh(jnp.dot(points, w_in, preferred_element_type=jnp.float32) + b_in).astype(
        jnp.bfloat16
    )
    pre = lax.dot_general(
        w_out, hidden, (((0,), (1,)), ((), ())), preferred_element_type=jnp.float32
    )
    hidden, scaled = (hidden, (pre * inv_scale[:, None]).astype(jnp.bfloat16))
    own_hidden = lax.dynamic_slice_in_dim(hidden, first, quarter, 0)
    own_pair = jnp.concatenate([solves, probes], axis=0)
    own_sq = jnp.sum(jnp.square(scaled.astype(jnp.float32)), axis=0)
    scaled32 = scaled.astype(jnp.float32)
    visitor = jnp.concatenate([scaled, probes, solves], axis=0)
    for bit in range(levels):
        moved = shifted(visitor, "blk", -(1 << bit))
        visitor = jnp.where(rep_index // (1 << bit) % 2 == 1, moved, visitor)

    def accumulate(state, vis):
        totals, pull = couple(scaled, own_pair, own_sq, vis, feat)
        return (state[0] + totals, state[1] + pull)

    init = (jnp.zeros((rows,), jnp.float32), jnp.zeros((feat, rows), jnp.float32))
    steps = blocks // reps
    behind = shifted(visitor, "blk", reps)

    def advance_both(index, carry):
        state, ahead_vis, behind_vis = carry
        state = accumulate(accumulate(state, ahead_vis), behind_vis)
        ahead_vis = shifted(ahead_vis, "blk", -reps)
        behind_vis = shifted(behind_vis, "blk", reps)
        return (state, ahead_vis, behind_vis)

    state, ahead_vis, behind_vis = lax.fori_loop(
        0, steps // 2 - 1, advance_both, (init, visitor, behind)
    )
    state = accumulate(accumulate(state, ahead_vis), behind_vis)
    totals, pull = state
    drift = pull - scaled32 * totals[None, :]
    summed = sum_at_owner(drift, "rep", 1)
    feat_grad = summed * inv_scale[:, None]
    grad_b16 = feat_grad.astype(jnp.bfloat16)
    back = lax.dot_general(
        grad_b16, w_out, (((0,), (1,)), ((), ())), preferred_element_type=jnp.float32
    )
    hid32 = own_hidden.astype(jnp.float32)
    pre_grad = back * (1.0 - hid32 * hid32)
    norm = 1.0 / math.sqrt(npts)
    term_w_in = (
        lax.dot_general(
            own_points,
            pre_grad.astype(jnp.bfloat16),
            (((0,), (0,)), ((), ())),
            preferred_element_type=jnp.float32,
        )
        * norm
    )
    term_b_in = jnp.sum(pre_grad, axis=0) * norm
    term_w_out = (
        lax.dot_general(
            own_hidden, grad_b16, (((0,), (1,)), ((), ())), preferred_element_type=jnp.float32
        )
        * norm
    )
    grad_w_in, grad_b_in, grad_w_out = lax.psum((term_w_in, term_b_in, term_w_out), ("blk", "rep"))
    return (feat_grad, grad_w_in, grad_b_in, grad_w_out)


def solution(mesh):
    in_specs = (P("blk", None), P(), P(), P(), P(), P(None, "blk"), P(None, "blk"))
    out_specs = (P(None, ("blk", "rep")), P(), P(), P())
    return jax.shard_map(
        on_device, mesh=mesh, in_specs=in_specs, out_specs=out_specs, check_vma=False
    )
```

profile of v0, /device:TPU:2, one launch (start us, length us, event | category | flops | bytes accessed | tf_op | source)
XLA Modules:
  0.0 443.5 jit_solution(13951835075255544906)
XLA Ops:
  7.2 1.4 copy-done
  8.6 2.2 tanh_convert_fusion
  11.7 1.0 fusion.13
  13.6 2.3 collective-permute-start.2
  16.0 6.5 %collective-permute-done.2 = bf16[192,768]{1,0:T(8,128)(2,1)S(1)} collective-permute-done((bf16[192,768]{1,0:T(8,128)(2,1)S(1)}, bf16[192,768]{1,0:T(8,128)(2,1)S(1)}, u32[]{:S(2)}, u32[]{:S(2)}) %collective-permute-start.2) | collective-permute-done | bytes 294944 | tf_op jit(solution)/shard_map/ppermute | solution.py:11
  23.4 12.7 %collective-permute-start.3 = (bf16[192,768]{1,0:T(8,128)(2,1)S(1)}, bf16[192,768]{1,0:T(8,128)(2,1)S(1)}, u32[]{:S(2)}, u32[]{:S(2)}) collective-permute-start(bf16[192,768]{1,0:T(8,128)(2,1)S(1)} %broadcast_select_fusion), channel_id=1, source_target_pairs={{8,0},{12,4},{16,8},{20,12},{24,16},{28,20},{32,24},{36,28},{40,32... | collective-permute-start | bytes 884744 | tf_op jit(solution)/shard_map/ppermute | solution.py:11
  36.2 5.4 %collective-permute-done.3 = bf16[192,768]{1,0:T(8,128)(2,1)S(1)} collective-permute-done((bf16[192,768]{1,0:T(8,128)(2,1)S(1)}, bf16[192,768]{1,0:T(8,128)(2,1)S(1)}, u32[]{:S(2)}, u32[]{:S(2)}) %collective-permute-start.3) | collective-permute-done | bytes 294944 | tf_op jit(solution)/shard_map/ppermute | solution.py:11
  42.3 9.3 %collective-permute-done.4 = bf16[192,768]{1,0:T(8,128)(2,1)} collective-permute-done((bf16[192,768]{1,0:T(8,128)(2,1)}, bf16[192,768]{1,0:T(8,128)(2,1)}, u32[]{:S(2)}, u32[]{:S(2)}) %collective-permute-start.4) | collective-permute-done | bytes 294944 | tf_op jit(solution)/shard_map/ppermute | solution.py:11
  51.7 93.9 %while.17 = (s32[]{:T(128)}, f32[768]{0:T(1024)S(1)}, f32[64,768]{1,0:T(8,128)}, bf16[192,768]{1,0:T(8,128)(2,1)}, bf16[192,768]{1,0:T(8,128)(2,1)}, /*index=5*/...) while((s32[]{:T(128)}, f32[768]{0:T(1024)S(1)}, ...), condition=%wide.region_6.7_spmd.clone, body=%wide.region_1.6_spmd.clone.sunk | while | flops 613858560 | bytes 20095168 | solution.py:87
  53.6 2.0 collective-permute-start.1
  56.7 1.8 convert_reduce_fusion.6
  58.5 1.0 convolution_bitcast_fusion.3
  59.5 1.8 convert_reduce_fusion.7
  61.3 1.9 fusion.79
  63.3 1.0 copy.23
  64.3 2.1 collective-permute-start
  68.4 1.8 convert_reduce_fusion.6
  70.3 1.0 convolution_bitcast_fusion.3
  71.3 1.8 convert_reduce_fusion.7
  73.1 2.0 fusion.79
  75.1 1.2 collective-permute-done.1
  77.3 3.0 collective-permute-start
  82.3 1.8 convert_reduce_fusion.6
  84.1 1.0 convolution_bitcast_fusion.3
  85.1 1.8 convert_reduce_fusion.7
  86.9 2.0 fusion.79
  89.0 1.2 collective-permute-done.1
  91.1 3.0 collective-permute-start
  96.1 1.8 convert_reduce_fusion.6
  97.9 1.0 convolution_bitcast_fusion.3
  98.9 1.8 convert_reduce_fusion.7
  100.8 2.0 fusion.79
  102.8 1.2 collective-permute-done.1
  104.9 3.0 collective-permute-start
  110.0 1.8 convert_reduce_fusion.6
  111.8 1.0 convolution_bitcast_fusion.3
  112.8 1.8 convert_reduce_fusion.7
  114.6 2.0 fusion.79
  116.7 1.2 collective-permute-done.1
  118.8 3.0 collective-permute-start
  123.8 1.8 convert_reduce_fusion.6
  125.6 1.0 convolution_bitcast_fusion.3
  126.7 1.8 convert_reduce_fusion.7
  128.5 2.0 fusion.79
  130.5 1.2 collective-permute-done.1
  132.6 3.0 collective-permute-start
  137.7 1.8 convert_reduce_fusion.6
  139.5 1.0 convolution_bitcast_fusion.3
  140.5 1.8 convert_reduce_fusion.7
  142.3 2.0 fusion.79
  144.4 1.2 collective-permute-done.1
  145.5 1.4 fusion.21
  147.0 1.0 multiply_reduce_fusion.2
  148.0 1.5 fusion.27
  149.4 1.8 convert_reduce_fusion.3
  151.3 1.2 fusion.25
  152.5 1.9 convert_reduce_fusion.2
  154.5 1.3 fusion.14
  156.8 4.1 all-to-all-start
  160.9 7.5 %all-to-all-done = f32[4,64,192]{2,1,0:T(8,128)S(1)} async-done(((f32[4,64,192]{2,1,0:T(8,128)}), f32[4,64,192]{2,1,0:T(8,128)S(1)}, u32[]{:S(2)}, u32[]{:S(2)}) %all-to-all-start) | async-done | bytes 196640 | tf_op jit(solution)/shard_map/all_to_all | solution.py:22
  169.6 1.8 convolution_multiply_fusion
  171.5 78.0 %psum.22 = f32[512]{0:T(512)} all-reduce(f32[512]{0:T(512)S(1)} %broadcast_multiply_fusion.1), channel_id=1, replica_groups=mesh['blk'=64,'rep'=4] {'blk','rep'}, use_global_device_ids=true, to_apply=%region_14.15 | all-reduce | flops 512 | bytes 4096 | tf_op jit(solution)/shard_map/psum | solution.py:118
  249.5 183.4 %all-reduce.3.cloned.1.call-done = (f32[1024,512]{1,0:T(8,128)}, f32[512,64]{0,1:T(8,128)}) async-done(((f32[1024,512]{1,0:T(8,128)}, f32[512,64]{0,1:T(8,128)}), (f32[1024,512]{1,0:T(8,128)}, f32[512,64]{0,1:T(8,128)})) %all-reduce.3.cloned.1.call-update) | async-done | bytes 2228240 | tf_op jit(solution)/shard_map/psum | solution.py:118
  432.9 3.1 copy.32
  (98 shorter events, 26.4 us)
Async XLA Ops:
  7.2 1.4 copy-start
  7.2 4.5 %copy-start.8 = (bf16[512,64]{0,1:T(8,128)(2,1)S(1)}, bf16[512,64]{0,1:T(8,128)(2,1)}, u32[]{:S(2)}) copy-start(bf16[512,64]{0,1:T(8,128)(2,1)} %param.12) | copy-start | bytes 196612
  7.2 4.5 %copy-start.10 = (f32[64]{0:T(128)S(1)}, f32[64]{0:T(128)}, u32[]{:S(2)}) copy-start(f32[64]{0:T(128)} %param.13) | copy-start | bytes 772
  7.2 5.5 %copy-start.4 = (bf16[64,768]{1,0:T(8,128)(2,1)S(1)}, bf16[64,768]{1,0:T(8,128)(2,1)}, u32[]{:S(2)}) copy-start(bf16[64,768]{1,0:T(8,128)(2,1)} %param.14) | copy-start | bytes 294916
  8.6 4.1 copy-start.5
  10.8 0.9 copy-start.2
  13.6 8.8 %collective-permute-start.2 = (bf16[192,768]{1,0:T(8,128)(2,1)S(1)}, bf16[192,768]{1,0:T(8,128)(2,1)S(1)}, u32[]{:S(2)}, u32[]{:S(2)}) collective-permute-start(bf16[192,768]{1,0:T(8,128)(2,1)S(1)} %pad_maximum_fusion), channel_id=1, source_target_pairs={{4,0},{8,4},{12,8},{16,12},{20,16},{24,20},{28,24},{32,28},{36,32}... | collective-permute-start | bytes 884744 | tf_op jit(solution)/shard_map/ppermute | solution.py:11
  23.4 18.1 %collective-permute-start.3 = (bf16[192,768]{1,0:T(8,128)(2,1)S(1)}, bf16[192,768]{1,0:T(8,128)(2,1)S(1)}, u32[]{:S(2)}, u32[]{:S(2)}) collective-permute-start(bf16[192,768]{1,0:T(8,128)(2,1)S(1)} %broadcast_select_fusion), channel_id=1, source_target_pairs={{8,0},{12,4},{16,8},{20,12},{24,16},{28,20},{32,24},{36,28},{40,32... | collective-permute-start | bytes 884744 | tf_op jit(solution)/shard_map/ppermute | solution.py:11
  42.3 9.4 %collective-permute-start.4 = (bf16[192,768]{1,0:T(8,128)(2,1)}, bf16[192,768]{1,0:T(8,128)(2,1)}, u32[]{:S(2)}, u32[]{:S(2)}) collective-permute-start(bf16[192,768]{1,0:T(8,128)(2,1)} %broadcast_select_fusion.1), channel_id=1, source_target_pairs={{240,0},{244,4},{248,8},{252,12},{0,16},{4,20},{8,24},{12,28},{16,... | collective-permute-start | bytes 884744 | tf_op jit(solution)/shard_map/ppermute | solution.py:11
  52.6 10.7 %collective-permute-start = (bf16[192,768]{1,0:T(8,128)(2,1)S(1)}, bf16[192,768]{1,0:T(8,128)(2,1)}, u32[]{:S(2)}, u32[]{:S(2)}) collective-permute-start(bf16[192,768]{1,0:T(8,128)(2,1)S(1)} %copy.23), channel_id=1, source_target_pairs={{16,0},{20,4},{24,8},{28,12},{32,16},{36,20},{40,24},{44,28},{48,3... | collective-permute-start | bytes 884744 | tf_op jit(solution)/shard_map/while/body/eval_jaxpr/ppermute | solution.py:11
  53.6 9.7 %collective-permute-start.1 = (bf16[192,768]{1,0:T(8,128)(2,1)S(1)}, bf16[192,768]{1,0:T(8,128)(2,1)}, u32[]{:S(2)}, u32[]{:S(2)}) collective-permute-start(bf16[192,768]{1,0:T(8,128)(2,1)S(1)} %copy.24), channel_id=1, source_target_pairs={{240,0},{244,4},{248,8},{252,12},{0,16},{4,20},{8,24},{12,28},{16,... | collective-permute-start | bytes 884744 | tf_op jit(solution)/shard_map/while/body/eval_jaxpr/ppermute | solution.py:11
  64.3 10.9 %collective-permute-start = (bf16[192,768]{1,0:T(8,128)(2,1)S(1)}, bf16[192,768]{1,0:T(8,128)(2,1)}, u32[]{:S(2)}, u32[]{:S(2)}) collective-permute-start(bf16[192,768]{1,0:T(8,128)(2,1)S(1)} %copy.23), channel_id=1, source_target_pairs={{16,0},{20,4},{24,8},{28,12},{32,16},{36,20},{40,24},{44,28},{48,3... | collective-permute-start | bytes 884744 | tf_op jit(solution)/shard_map/while/body/eval_jaxpr/ppermute | solution.py:11
  67.4 8.9 %collective-permute-start.1 = (bf16[192,768]{1,0:T(8,128)(2,1)S(1)}, bf16[192,768]{1,0:T(8,128)(2,1)}, u32[]{:S(2)}, u32[]{:S(2)}) collective-permute-start(bf16[192,768]{1,0:T(8,128)(2,1)S(1)} %copy.24), channel_id=1, source_target_pairs={{240,0},{244,4},{248,8},{252,12},{0,16},{4,20},{8,24},{12,28},{16,... | collective-permute-start | bytes 884744 | tf_op jit(solution)/shard_map/while/body/eval_jaxpr/ppermute | solution.py:11
  77.3 11.7 %collective-permute-start = (bf16[192,768]{1,0:T(8,128)(2,1)S(1)}, bf16[192,768]{1,0:T(8,128)(2,1)}, u32[]{:S(2)}, u32[]{:S(2)}) collective-permute-start(bf16[192,768]{1,0:T(8,128)(2,1)S(1)} %copy.23), channel_id=1, source_target_pairs={{16,0},{20,4},{24,8},{28,12},{32,16},{36,20},{40,24},{44,28},{48,3... | collective-permute-start | bytes 884744 | tf_op jit(solution)/shard_map/while/body/eval_jaxpr/ppermute | solution.py:11
  81.2 8.9 %collective-permute-start.1 = (bf16[192,768]{1,0:T(8,128)(2,1)S(1)}, bf16[192,768]{1,0:T(8,128)(2,1)}, u32[]{:S(2)}, u32[]{:S(2)}) collective-permute-start(bf16[192,768]{1,0:T(8,128)(2,1)S(1)} %copy.24), channel_id=1, source_target_pairs={{240,0},{244,4},{248,8},{252,12},{0,16},{4,20},{8,24},{12,28},{16,... | collective-permute-start | bytes 884744 | tf_op jit(solution)/shard_map/while/body/eval_jaxpr/ppermute | solution.py:11
  91.1 11.7 %collective-permute-start = (bf16[192,768]{1,0:T(8,128)(2,1)S(1)}, bf16[192,768]{1,0:T(8,128)(2,1)}, u32[]{:S(2)}, u32[]{:S(2)}) collective-permute-start(bf16[192,768]{1,0:T(8,128)(2,1)S(1)} %copy.23), channel_id=1, source_target_pairs={{16,0},{20,4},{24,8},{28,12},{32,16},{36,20},{40,24},{44,28},{48,3... | collective-permute-start | bytes 884744 | tf_op jit(solution)/shard_map/while/body/eval_jaxpr/ppermute | solution.py:11
  95.0 8.9 %collective-permute-start.1 = (bf16[192,768]{1,0:T(8,128)(2,1)S(1)}, bf16[192,768]{1,0:T(8,128)(2,1)}, u32[]{:S(2)}, u32[]{:S(2)}) collective-permute-start(bf16[192,768]{1,0:T(8,128)(2,1)S(1)} %copy.24), channel_id=1, source_target_pairs={{240,0},{244,4},{248,8},{252,12},{0,16},{4,20},{8,24},{12,28},{16,... | collective-permute-start | bytes 884744 | tf_op jit(solution)/shard_map/while/body/eval_jaxpr/ppermute | solution.py:11
  104.9 11.7 %collective-permute-start = (bf16[192,768]{1,0:T(8,128)(2,1)S(1)}, bf16[192,768]{1,0:T(8,128)(2,1)}, u32[]{:S(2)}, u32[]{:S(2)}) collective-permute-start(bf16[192,768]{1,0:T(8,128)(2,1)S(1)} %copy.23), channel_id=1, source_target_pairs={{16,0},{20,4},{24,8},{28,12},{32,16},{36,20},{40,24},{44,28},{48,3... | collective-permute-start | bytes 884744 | tf_op jit(solution)/shard_map/while/body/eval_jaxpr/ppermute | solution.py:11
  108.9 8.9 %collective-permute-start.1 = (bf16[192,768]{1,0:T(8,128)(2,1)S(1)}, bf16[192,768]{1,0:T(8,128)(2,1)}, u32[]{:S(2)}, u32[]{:S(2)}) collective-permute-start(bf16[192,768]{1,0:T(8,128)(2,1)S(1)} %copy.24), channel_id=1, source_target_pairs={{240,0},{244,4},{248,8},{252,12},{0,16},{4,20},{8,24},{12,28},{16,... | collective-permute-start | bytes 884744 | tf_op jit(solution)/shard_map/while/body/eval_jaxpr/ppermute | solution.py:11
  118.8 11.7 %collective-permute-start = (bf16[192,768]{1,0:T(8,128)(2,1)S(1)}, bf16[192,768]{1,0:T(8,128)(2,1)}, u32[]{:S(2)}, u32[]{:S(2)}) collective-permute-start(bf16[192,768]{1,0:T(8,128)(2,1)S(1)} %copy.23), channel_id=1, source_target_pairs={{16,0},{20,4},{24,8},{28,12},{32,16},{36,20},{40,24},{44,28},{48,3... | collective-permute-start | bytes 884744 | tf_op jit(solution)/shard_map/while/body/eval_jaxpr/ppermute | solution.py:11
  122.7 8.9 %collective-permute-start.1 = (bf16[192,768]{1,0:T(8,128)(2,1)S(1)}, bf16[192,768]{1,0:T(8,128)(2,1)}, u32[]{:S(2)}, u32[]{:S(2)}) collective-permute-start(bf16[192,768]{1,0:T(8,128)(2,1)S(1)} %copy.24), channel_id=1, source_target_pairs={{240,0},{244,4},{248,8},{252,12},{0,16},{4,20},{8,24},{12,28},{16,... | collective-permute-start | bytes 884744 | tf_op jit(solution)/shard_map/while/body/eval_jaxpr/ppermute | solution.py:11
  132.6 11.7 %collective-permute-start = (bf16[192,768]{1,0:T(8,128)(2,1)S(1)}, bf16[192,768]{1,0:T(8,128)(2,1)}, u32[]{:S(2)}, u32[]{:S(2)}) collective-permute-start(bf16[192,768]{1,0:T(8,128)(2,1)S(1)} %copy.23), channel_id=1, source_target_pairs={{16,0},{20,4},{24,8},{28,12},{32,16},{36,20},{40,24},{44,28},{48,3... | collective-permute-start | bytes 884744 | tf_op jit(solution)/shard_map/while/body/eval_jaxpr/ppermute | solution.py:11
  136.6 8.9 %collective-permute-start.1 = (bf16[192,768]{1,0:T(8,128)(2,1)S(1)}, bf16[192,768]{1,0:T(8,128)(2,1)}, u32[]{:S(2)}, u32[]{:S(2)}) collective-permute-start(bf16[192,768]{1,0:T(8,128)(2,1)S(1)} %copy.24), channel_id=1, source_target_pairs={{240,0},{244,4},{248,8},{252,12},{0,16},{4,20},{8,24},{12,28},{16,... | collective-permute-start | bytes 884744 | tf_op jit(solution)/shard_map/while/body/eval_jaxpr/ppermute | solution.py:11
  152.5 1.9 copy-start.1
  154.4 14.0 %copy-start.11 = (f32[64]{0:T(128)S(1)}, f32[64]{0:T(128)}, u32[]{:S(2)}) copy-start(f32[64]{0:T(128)} %param.13) | copy-start | bytes 772
  154.4 14.1 %copy-start.3 = (bf16[768,512]{1,0:T(8,128)(2,1)S(1)}, bf16[768,512]{1,0:T(8,128)(2,1)}, u32[]{:S(2)}) copy-start(bf16[768,512]{1,0:T(8,128)(2,1)} %copy-done.2) | copy-start | bytes 2359300
  154.4 14.1 %copy-start.9 = (bf16[512,64]{0,1:T(8,128)(2,1)S(1)}, bf16[512,64]{0,1:T(8,128)(2,1)}, u32[]{:S(2)}) copy-start(bf16[512,64]{0,1:T(8,128)(2,1)} %param.12) | copy-start | bytes 196612
  156.8 11.7 %all-to-all-start = ((f32[4,64,192]{2,1,0:T(8,128)}), f32[4,64,192]{2,1,0:T(8,128)S(1)}, u32[]{:S(2)}, u32[]{:S(2)}) async-start(f32[4,64,192]{2,1,0:T(8,128)} %bitcast.31), calls=%async_computation | async-start | bytes 524288 | tf_op jit(solution)/shard_map/all_to_all | solution.py:22
  160.9 272.0 %all-reduce.3.cloned.1.call-start = ((), (), s32[]{:S(2)}) async-start(), calls=%async_computation.1 | async-start | bytes 4456448 | tf_op jit(solution)/shard_map/psum | solution.py:118
  168.5 2.9 copy-start.6
  432.9 3.1 copy-start.7
Sparse Core Ops, SparseCore 0:
  171.6 261.2 all-reduce.2
where the time goes:
time: 445 us; the launch traced here: 443 us
  waiting for transfers between devices  219 us (49%)
  blocking collectives  78 us (18%)
  matrix products  68.9 us (15%)
  starting transfers between devices  38.3 us (9%)
  local copies, waits for them, and re-layouts  20.5 us (5%)
  between operations  14.2 us (3%)
    psum x1, waiting for transfers between devices, on_device(): lax.psum((term_w_in, term_b_in, term_w_out), ('blk', 'rep'))  183 us
    psum x1, blocking collectives, on_device(): lax.psum((term_w_in, term_b_in, term_w_out), ('blk', 'rep'))  78 us
    ppermute x17, starting transfers between devices, shifted(): return lax.ppermute(block, axis, route)  34.2 us
    ppermute x17, waiting for transfers between devices, shifted(): return lax.ppermute(block, axis, route)  28.2 us
    dot_general x16, matrix products, couple(): lax.dot_general(own_y, vis_y, (((0,), (0,)), ((), ())), preferred_element...  28.1 us
    dot_general x16, matrix products, couple(): lax.dot_general(vis_y, weight_b, (((1,), (1,)), ((), ())), preferred_elem...  23.8 us
    while x14, local copies, waits for them, and re-layouts  13.5 us
    dot_general x16, matrix products, couple(): lax.dot_general(own_pair, vis_pair, (((0,), (0,)), ((), ())), preferred_e...  10.8 us
  transfers between devices with their start and end apart: 19, of which 11 were waited for; matrix products, arithmetic and copies ran while one was open for 14% of the time, Pallas kernels for 0%

commit v1 on v0

--- a/solution.py
+++ b/solution.py
@@ -115,7 +115,9 @@
         )
         * norm
     )
-    grad_w_in, grad_b_in, grad_w_out = lax.psum((term_w_in, term_b_in, term_w_out), ("blk", "rep"))
+    grad_w_in, grad_b_in, grad_w_out = lax.psum(
+        lax.psum((term_w_in, term_b_in, term_w_out), "blk"), "rep"
+    )
     return (feat_grad, grad_w_in, grad_b_in, grad_w_out)
 
 

time: 445 us -> 944 us (2.12)
  waiting for transfers between devices: 219 us -> 630 us
  blocking collectives: 78 us -> 163 us
    psum x1 -> x2, waiting for transfers between devices: 183 us -> 594 us  [the longest x1 594 us: on_device(): lax.psum((term_w_in, term_b_in, term_w_out), 'blk')]
    psum x1 -> x2, blocking collectives: 78 us -> 163 us  [the longest x1 156 us: on_device(): lax.psum((term_w_in, term_b_in, term_w_out), 'blk')]
  transfers between devices with their start and end apart: 19 -> 20, of which waited for: 11 -> 11; matrix products, arithmetic and copies ran while one was open for 14% -> 6% of each run, Pallas kernels for 0% -> 0%
where the time goes in v1:
time: 944 us; the launch traced here: 939 us
  waiting for transfers between devices  630 us (67%)
  blocking collectives  163 us (17%)
  matrix products  68.9 us (7%)
  starting transfers between devices  38.3 us (4%)
  local copies, waits for them, and re-layouts  20.5 us (2%)
  between operations  14.2 us (2%)
    psum x1, waiting for transfers between devices, on_device(): lax.psum((term_w_in, term_b_in, term_w_out), 'blk')  594 us
    psum x1, blocking collectives, on_device(): lax.psum((term_w_in, term_b_in, term_w_out), 'blk')  156 us
    ppermute x17, starting transfers between devices, shifted(): return lax.ppermute(block, axis, route)  34.2 us
    ppermute x17, waiting for transfers between devices, shifted(): return lax.ppermute(block, axis, route)  28.2 us
    dot_general x16, matrix products, couple(): lax.dot_general(own_y, vis_y, (((0,), (0,)), ((), ())), preferred_element...  28.1 us
    dot_general x16, matrix products, couple(): lax.dot_general(vis_y, weight_b, (((1,), (1,)), ((), ())), preferred_elem...  23.8 us
  transfers between devices with their start and end apart: 20, of which 11 were waited for; matrix products, arithmetic and copies ran while one was open for 6% of the time, Pallas kernels for 0%

profile of v1, /device:TPU:2, one launch (start us, length us, event | category | flops | bytes accessed | tf_op | source)
XLA Modules:
  0.0 939.4 jit_solution(9417098722808379717)
XLA Ops:
  7.2 1.4 copy-done
  8.6 2.2 tanh_convert_fusion
  11.7 1.0 fusion.13
  13.6 2.3 collective-permute-start.2
  16.0 6.5 collective-permute-done.2
  23.4 12.7 %collective-permute-start.3 = (bf16[192,768]{1,0:T(8,128)(2,1)S(1)}, bf16[192,768]{1,0:T(8,128)(2,1)S(1)}, u32[]{:S(2)}, u32[]{:S(2)}) collective-permute-start(bf16[192,768]{1,0:T(8,128)(2,1)S(1)} %broadcast_select_fusion), channel_id=1, source_target_pairs={{8,0},{12,4},{16,8},{20,12},{24,16},{28,20},{32,24},{36,28},{40,32... | collective-permute-start | bytes 884744 | tf_op jit(solution)/shard_map/ppermute | solution.py:11
  36.2 5.4 collective-permute-done.3
  42.3 9.3 collective-permute-done.4
  51.7 93.9 %while.17 = (s32[]{:T(128)}, f32[768]{0:T(1024)S(1)}, f32[64,768]{1,0:T(8,128)}, bf16[192,768]{1,0:T(8,128)(2,1)}, bf16[192,768]{1,0:T(8,128)(2,1)}, /*index=5*/...) while((s32[]{:T(128)}, f32[768]{0:T(1024)S(1)}, ...), condition=%wide.region_6.7_spmd.clone, body=%wide.region_1.6_spmd.clone.sunk | while | flops 613858560 | bytes 20095168 | solution.py:87
  53.6 2.0 collective-permute-start.1
  56.7 1.8 convert_reduce_fusion.6
  58.5 1.0 convolution_bitcast_fusion.3
  59.5 1.8 convert_reduce_fusion.7
  61.3 1.9 fusion.79
  64.3 2.1 collective-permute-start
  68.4 1.8 convert_reduce_fusion.6
  70.3 1.0 convolution_bitcast_fusion.3
  71.3 1.8 convert_reduce_fusion.7
  73.1 2.0 fusion.79
  75.1 1.2 collective-permute-done.1
  77.3 3.0 collective-permute-start
  82.3 1.8 convert_reduce_fusion.6
  84.1 1.0 convolution_bitcast_fusion.3
  85.1 1.8 convert_reduce_fusion.7
  86.9 2.0 fusion.79
  89.0 1.2 collective-permute-done.1
  91.1 3.0 collective-permute-start
  96.1 1.8 convert_reduce_fusion.6
  97.9 1.0 convolution_bitcast_fusion.3
  98.9 1.8 convert_reduce_fusion.7
  100.8 2.0 fusion.79
  102.8 1.2 collective-permute-done.1
  104.9 3.0 collective-permute-start
  110.0 1.8 convert_reduce_fusion.6
  111.8 1.0 convolution_bitcast_fusion.3
  112.8 1.8 convert_reduce_fusion.7
  114.6 2.0 fusion.79
  116.7 1.2 collective-permute-done.1
  118.8 3.0 collective-permute-start
  123.8 1.8 convert_reduce_fusion.6
  125.6 1.0 convolution_bitcast_fusion.3
  126.7 1.8 convert_reduce_fusion.7
  128.5 2.0 fusion.79
  130.5 1.2 collective-permute-done.1
  132.6 3.0 collective-permute-start
  137.7 1.8 convert_reduce_fusion.6
  139.5 1.0 convolution_bitcast_fusion.3
  140.5 1.8 convert_reduce_fusion.7
  142.3 2.0 fusion.79
  144.4 1.2 collective-permute-done.1
  145.5 1.4 fusion.21
  147.0 1.0 multiply_reduce_fusion.2
  148.0 1.5 fusion.27
  149.4 1.8 convert_reduce_fusion.3
  151.3 1.2 fusion.25
  152.5 1.9 convert_reduce_fusion.2
  154.5 1.3 fusion.14
  156.8 4.1 all-to-all-start
  160.9 7.5 all-to-all-done
  169.6 1.8 convolution_multiply_fusion
  171.5 593.9 %all-reduce.5.cloned.1.call-done = (f32[1024,512]{1,0:T(8,128)}, f32[512,64]{0,1:T(8,128)}) async-done(((f32[1024,512]{1,0:T(8,128)}, f32[512,64]{0,1:T(8,128)}), (f32[1024,512]{1,0:T(8,128)}, f32[512,64]{0,1:T(8,128)})) %all-reduce.5.cloned.1.call-update) | async-done | bytes 2228240 | tf_op jit(solution)/shard_map/psum | solution.py:119
  765.5 155.6 %psum.44 = f32[512]{0:T(512)S(1)} all-reduce(f32[512]{0:T(512)S(1)} %broadcast_multiply_fusion.1), channel_id=1, replica_groups=mesh['blk'=64,'rep'=4] {'blk'}, use_global_device_ids=true, to_apply=%region_15.16 | all-reduce | flops 512 | bytes 4096 | tf_op jit(solution)/shard_map/psum | solution.py:119
  921.1 7.7 psum.45
  928.8 3.1 copy.34
  (102 shorter events, 27.4 us)
Async XLA Ops:
  7.2 1.4 copy-start
  7.2 4.5 copy-start.8
  7.2 4.5 copy-start.10
  7.2 5.5 copy-start.4
  8.6 4.1 copy-start.5
  10.8 0.9 copy-start.2
  13.6 8.8 collective-permute-start.2
  23.4 18.1 %collective-permute-start.3 = (bf16[192,768]{1,0:T(8,128)(2,1)S(1)}, bf16[192,768]{1,0:T(8,128)(2,1)S(1)}, u32[]{:S(2)}, u32[]{:S(2)}) collective-permute-start(bf16[192,768]{1,0:T(8,128)(2,1)S(1)} %broadcast_select_fusion), channel_id=1, source_target_pairs={{8,0},{12,4},{16,8},{20,12},{24,16},{28,20},{32,24},{36,28},{40,32... | collective-permute-start | bytes 884744 | tf_op jit(solution)/shard_map/ppermute | solution.py:11
  42.3 9.4 collective-permute-start.4
  52.6 10.7 %collective-permute-start = (bf16[192,768]{1,0:T(8,128)(2,1)S(1)}, bf16[192,768]{1,0:T(8,128)(2,1)}, u32[]{:S(2)}, u32[]{:S(2)}) collective-permute-start(bf16[192,768]{1,0:T(8,128)(2,1)S(1)} %copy.23), channel_id=1, source_target_pairs={{16,0},{20,4},{24,8},{28,12},{32,16},{36,20},{40,24},{44,28},{48,3... | collective-permute-start | bytes 884744 | tf_op jit(solution)/shard_map/while/body/eval_jaxpr/ppermute | solution.py:11
  53.6 9.7 %collective-permute-start.1 = (bf16[192,768]{1,0:T(8,128)(2,1)S(1)}, bf16[192,768]{1,0:T(8,128)(2,1)}, u32[]{:S(2)}, u32[]{:S(2)}) collective-permute-start(bf16[192,768]{1,0:T(8,128)(2,1)S(1)} %copy.24), channel_id=1, source_target_pairs={{240,0},{244,4},{248,8},{252,12},{0,16},{4,20},{8,24},{12,28},{16,... | collective-permute-start | bytes 884744 | tf_op jit(solution)/shard_map/while/body/eval_jaxpr/ppermute | solution.py:11
  64.3 10.9 %collective-permute-start = (bf16[192,768]{1,0:T(8,128)(2,1)S(1)}, bf16[192,768]{1,0:T(8,128)(2,1)}, u32[]{:S(2)}, u32[]{:S(2)}) collective-permute-start(bf16[192,768]{1,0:T(8,128)(2,1)S(1)} %copy.23), channel_id=1, source_target_pairs={{16,0},{20,4},{24,8},{28,12},{32,16},{36,20},{40,24},{44,28},{48,3... | collective-permute-start | bytes 884744 | tf_op jit(solution)/shard_map/while/body/eval_jaxpr/ppermute | solution.py:11
  67.4 8.9 collective-permute-start.1
  77.3 11.7 %collective-permute-start = (bf16[192,768]{1,0:T(8,128)(2,1)S(1)}, bf16[192,768]{1,0:T(8,128)(2,1)}, u32[]{:S(2)}, u32[]{:S(2)}) collective-permute-start(bf16[192,768]{1,0:T(8,128)(2,1)S(1)} %copy.23), channel_id=1, source_target_pairs={{16,0},{20,4},{24,8},{28,12},{32,16},{36,20},{40,24},{44,28},{48,3... | collective-permute-start | bytes 884744 | tf_op jit(solution)/shard_map/while/body/eval_jaxpr/ppermute | solution.py:11
  81.2 8.9 collective-permute-start.1
  91.1 11.7 %collective-permute-start = (bf16[192,768]{1,0:T(8,128)(2,1)S(1)}, bf16[192,768]{1,0:T(8,128)(2,1)}, u32[]{:S(2)}, u32[]{:S(2)}) collective-permute-start(bf16[192,768]{1,0:T(8,128)(2,1)S(1)} %copy.23), channel_id=1, source_target_pairs={{16,0},{20,4},{24,8},{28,12},{32,16},{36,20},{40,24},{44,28},{48,3... | collective-permute-start | bytes 884744 | tf_op jit(solution)/shard_map/while/body/eval_jaxpr/ppermute | solution.py:11
  95.0 8.9 collective-permute-start.1
  104.9 11.7 %collective-permute-start = (bf16[192,768]{1,0:T(8,128)(2,1)S(1)}, bf16[192,768]{1,0:T(8,128)(2,1)}, u32[]{:S(2)}, u32[]{:S(2)}) collective-permute-start(bf16[192,768]{1,0:T(8,128)(2,1)S(1)} %copy.23), channel_id=1, source_target_pairs={{16,0},{20,4},{24,8},{28,12},{32,16},{36,20},{40,24},{44,28},{48,3... | collective-permute-start | bytes 884744 | tf_op jit(solution)/shard_map/while/body/eval_jaxpr/ppermute | solution.py:11
  108.9 8.9 collective-permute-start.1
  118.8 11.7 %collective-permute-start = (bf16[192,768]{1,0:T(8,128)(2,1)S(1)}, bf16[192,768]{1,0:T(8,128)(2,1)}, u32[]{:S(2)}, u32[]{:S(2)}) collective-permute-start(bf16[192,768]{1,0:T(8,128)(2,1)S(1)} %copy.23), channel_id=1, source_target_pairs={{16,0},{20,4},{24,8},{28,12},{32,16},{36,20},{40,24},{44,28},{48,3... | collective-permute-start | bytes 884744 | tf_op jit(solution)/shard_map/while/body/eval_jaxpr/ppermute | solution.py:11
  122.7 8.9 collective-permute-start.1
  132.6 11.7 %collective-permute-start = (bf16[192,768]{1,0:T(8,128)(2,1)S(1)}, bf16[192,768]{1,0:T(8,128)(2,1)}, u32[]{:S(2)}, u32[]{:S(2)}) collective-permute-start(bf16[192,768]{1,0:T(8,128)(2,1)S(1)} %copy.23), channel_id=1, source_target_pairs={{16,0},{20,4},{24,8},{28,12},{32,16},{36,20},{40,24},{44,28},{48,3... | collective-permute-start | bytes 884744 | tf_op jit(solution)/shard_map/while/body/eval_jaxpr/ppermute | solution.py:11
  136.6 8.9 collective-permute-start.1
  152.5 1.9 copy-start.1
  154.4 14.0 %copy-start.11 = (f32[64]{0:T(128)S(1)}, f32[64]{0:T(128)}, u32[]{:S(2)}) copy-start(f32[64]{0:T(128)} %param.13) | copy-start | bytes 772
  154.4 14.1 %copy-start.3 = (bf16[768,512]{1,0:T(8,128)(2,1)S(1)}, bf16[768,512]{1,0:T(8,128)(2,1)}, u32[]{:S(2)}) copy-start(bf16[768,512]{1,0:T(8,128)(2,1)} %copy-done.2) | copy-start | bytes 2359300
  154.4 14.1 %copy-start.9 = (bf16[512,64]{0,1:T(8,128)(2,1)S(1)}, bf16[512,64]{0,1:T(8,128)(2,1)}, u32[]{:S(2)}) copy-start(bf16[512,64]{0,1:T(8,128)(2,1)} %param.12) | copy-start | bytes 196612
  156.8 11.7 %all-to-all-start = ((f32[4,64,192]{2,1,0:T(8,128)}), f32[4,64,192]{2,1,0:T(8,128)S(1)}, u32[]{:S(2)}, u32[]{:S(2)}) async-start(f32[4,64,192]{2,1,0:T(8,128)} %bitcast.31), calls=%async_computation | async-start | bytes 524288 | tf_op jit(solution)/shard_map/all_to_all | solution.py:22
  160.9 604.5 %all-reduce.5.cloned.1.call-start = ((), (), s32[]{:S(2)}) async-start(), calls=%async_computation.1 | async-start | bytes 4456448 | tf_op jit(solution)/shard_map/psum | solution.py:119
  168.5 2.9 copy-start.6
  171.5 757.3 %all-reduce.7.cloned.1.call-start = ((), (), s32[]{:S(2)}) async-start(), calls=%async_computation.2 | async-start | bytes 4456448 | tf_op jit(solution)/shard_map/psum | solution.py:118
  928.8 3.1 copy-start.7
Sparse Core Ops, SparseCore 0:
  171.6 593.8 all-reduce.4
  768.4 65.2 all-reduce.6
